TPU v7x, 512 devices: a whole 4x8x8 slice. The times are simulated.
512 devices in a mesh: shot: 16 (over x, z_lo), blk: 32 (over z_hi, y, core).
Axes of the slice: x: 4, y: 8, z: 8 (z_hi: 2, z_lo: 4; z = z_hi * 4 + z_lo), core: 2. Of those that a mesh axis runs over, the one named last changes fastest.
Arguments:
- state_before: float32 [16, 256, 64, 128], P('shot', 'blk'), may hold values from -7 to 7
- state_now: float32 [16, 256, 64, 128], P('shot', 'blk'), may hold values from -7 to 7
- adjoint_later: float32 [16, 256, 64, 128], P('shot', 'blk'), may hold values from -7 to 7
- adjoint_now: float32 [16, 256, 64, 128], P('shot', 'blk'), may hold values from -7 to 7
- courant_sq: float32 [256, 128, 128], P('blk', 'shot'), may hold values from 0.02 to 0.3
- epsilon: float32 [256, 128, 128], P('blk', 'shot'), may hold values from 0.02 to 0.3
- tilt_angle: float32 [256, 128, 128], P('blk', 'shot'), may hold values from 0 to 1.2
- azimuth: float32 [256, 128, 128], P('blk', 'shot'), may hold values from -3.140625 to 3.140625
- aperture_anchor: int32 [16], P('shot'), may hold values from 0 to 64, as said below
- step_index: int32 [1], replicated, may hold values from 0 to 12
- wavelet: float32 [16, 16], P('shot'), may hold values from -8 to 8
- residual_traces: float32 [16, 16, 128], P('shot'), may hold values from -6 to 6
- source_x: int32 [16], P('shot'), may hold values from 0 to 255
- source_y: int32 [16], P('shot'), may hold values from 0 to 63
- source_z: int32 [16], P('shot'), may hold values from 0 to 127
- receiver_x: int32 [16, 128], P('shot'), may hold values from 0 to 255
- receiver_y: int32 [16, 128], P('shot'), may hold values from 0 to 63
- receiver_z: int32 [16, 128], P('shot'), may hold values from 0 to 127
Outputs:
- adjoint_one: float32 [16, 256, 64, 128], P('shot', 'blk')
- adjoint_zero: float32 [16, 256, 64, 128], P('shot', 'blk')
- model_grad: float32 [256, 128, 128], P('blk', 'shot')
Inputs may be any that keep to these rules, and one draw needn't show every extreme that they name: `aperture_anchor`: each value is a multiple of 8; some shot has 0 and some shot has 64.
All inputs are finite; a program needn't handle non-finite values.
Results may differ from a plain program's by a relative error of at most 0.0003.
Values sent between devices are 32-bit elements; how exact they have to be, the bound alone decides.
A program may use at most 64 MiB of HBM per device.

v0:
```python
import jax
import jax.numpy as jnp
from jax import lax
from jax.sharding import PartitionSpec as P

STEPS = 4
COEF = (0.8, -0.2, 4.0 / 105.0, -1.0 / 280.0)


def padded_2(array, sides, width):
    for axis, dim in sides:
        size, length = (lax.axis_size(axis), array.shape[dim])
        up = [(i, (i + 1) % size) for i in range(size - 1)]
        down = [(j, i) for i, j in up]
        last = lax.slice_in_dim(array, length - width, length, axis=dim)
        leading = lax.slice_in_dim(array, 0, width, axis=dim)
        before = lax.ppermute(last, axis, up)
        after = lax.ppermute(leading, axis, down)
        array = jnp.concatenate([before, array, after], axis=dim)
    return array


def first_diff(padded, axis, count):
    summed = None
    for k in range(1, 5):
        upper_part = lax.slice_in_dim(padded, 4 + k, 4 + k + count, axis=axis)
        lower_part = lax.slice_in_dim(padded, 4 - k, 4 - k + count, axis=axis)
        addend = COEF[k - 1] * (upper_part - lower_part)
        summed = addend if summed is None else summed + addend
    return summed


def pad_axis(field, axis):
    widths = [(0, 0), (0, 0), (0, 0)]
    widths[axis] = (4, 4)
    return jnp.pad(field, widths)


def operate_shallow(field, tensor_parts):
    twice_eps, normal_x, normal_y, normal_z = tensor_parts
    rows = field.shape[0]
    extended = padded_2(field, (("blk", 0),), 4)
    slope_x = first_diff(extended, 0, rows)
    slope_y = first_diff(pad_axis(field, 1), 1, field.shape[1])
    slope_z = first_diff(pad_axis(field, 2), 2, field.shape[2])
    normal_slope = normal_x * slope_x + normal_y * slope_y + normal_z * slope_z
    flux_x = (1.0 + twice_eps) * slope_x - twice_eps * normal_x * normal_slope
    flux_y = (1.0 + twice_eps) * slope_y - twice_eps * normal_y * normal_slope
    flux_z = (1.0 + twice_eps) * slope_z - twice_eps * normal_z * normal_slope
    flux_ext = padded_2(flux_x, (("blk", 0),), 4)
    result = first_diff(flux_ext, 0, rows)
    result = result + first_diff(pad_axis(flux_y, 1), 1, field.shape[1])
    return result + first_diff(pad_axis(flux_z, 2), 2, field.shape[2])


def on_device(
    state_before,
    state_now,
    adjoint_later,
    adjoint_now,
    courant_sq,
    epsilon,
    tilt_angle,
    azimuth,
    aperture_anchor,
    step_index,
    wavelet,
    residual_traces,
    source_x,
    source_y,
    source_z,
    receiver_x,
    receiver_y,
    receiver_z,
):
    rows = state_now.shape[1]
    width_y = state_now.shape[2]
    depth = state_now.shape[3]
    block_index = lax.axis_index("blk")
    anchor = aperture_anchor[0]
    start_step = step_index[0]
    empty = jnp.zeros((rows, width_y, depth), jnp.float32)
    carried = (empty, empty, empty, empty)
    pieces = (
        lax.all_gather(courant_sq, "shot", axis=1, tiled=True),
        lax.all_gather(epsilon, "shot", axis=1, tiled=True),
        lax.all_gather(tilt_angle, "shot", axis=1, tiled=True),
        lax.all_gather(azimuth, "shot", axis=1, tiled=True),
    )
    count = pieces[0].shape[1]
    relative = jnp.int32(0) - anchor
    inside = (relative > -count) & (relative < width_y)
    offset = jnp.clip(relative + count, 0, width_y + count)
    placed = []
    for held, piece in zip(carried, pieces):
        spread = jnp.zeros((rows, width_y + 2 * count, depth), jnp.float32)
        spread = lax.dynamic_update_slice(spread, piece, (0, offset, 0))
        placed.append(jnp.where(inside, spread[:, count : count + width_y], 0.0))
    speed_term, eps_part, tilt_part, azimuth_part = tuple(placed)
    twice_eps = 2.0 * eps_part
    tensor_parts = (
        twice_eps,
        jnp.sin(tilt_part) * jnp.cos(azimuth_part),
        jnp.sin(tilt_part) * jnp.sin(azimuth_part),
        jnp.cos(tilt_part),
    )

    def operate(field):
        return operate_shallow(field, tensor_parts)

    global_x = block_index * rows + lax.broadcasted_iota(jnp.int32, (rows, width_y, depth), 0)
    cell_y = lax.broadcasted_iota(jnp.int32, (rows, width_y, depth), 1)
    cell_z = lax.broadcasted_iota(jnp.int32, (rows, width_y, depth), 2)
    source_mask = (global_x == source_x[0]) & (cell_y == source_y[0]) & (cell_z == source_z[0])
    local_rows = receiver_x[0] - block_index * rows
    plane_index = local_rows * width_y + receiver_y[0]
    receiver_inside = (local_rows >= 0) & (local_rows < rows)
    plane_pick = (
        (
            lax.broadcasted_iota(jnp.int32, (rows * width_y, plane_index.shape[0]), 0)
            == plane_index[None, :]
        )
        & receiver_inside[None, :]
    ).astype(jnp.float32)
    depth_match = (
        lax.broadcasted_iota(jnp.int32, (plane_index.shape[0], depth), 1) == receiver_z[0][:, None]
    ).astype(jnp.float32)
    previous = state_before[0]
    current = state_now[0]
    images = []
    for t in range(STEPS):
        image = operate(current)
        images.append(image)
        if t < STEPS - 1:
            amplitude = lax.dynamic_index_in_dim(wavelet[0], start_step + t, keepdims=False)
            following = 2.0 * current - previous + speed_term * image
            following = following + jnp.where(source_mask, amplitude, 0.0)
            previous, current = (current, following)
    later = adjoint_later[0]
    present = adjoint_now[0]
    shot_grad = jnp.zeros((rows, width_y, depth), jnp.float32)
    for t in reversed(range(STEPS)):
        shot_grad = shot_grad + present * images[t]
        earlier = 2.0 * present - later + operate(speed_term * present)
        samples = lax.dynamic_index_in_dim(residual_traces[0], start_step + t, keepdims=False)
        depth_pick = depth_match * samples[:, None]
        injected = jnp.dot(
            plane_pick,
            depth_pick,
            precision=lax.Precision.HIGHEST,
            preferred_element_type=jnp.float32,
        )
        earlier = earlier + injected.reshape(rows, width_y, depth)
        later, present = (present, earlier)
    grad_slab = jnp.zeros((rows, 2 * width_y, depth), jnp.float32)
    grad_slab = lax.dynamic_update_slice(grad_slab, shot_grad, (0, anchor, 0))
    model_grad = lax.psum_scatter(grad_slab, "shot", scatter_dimension=1, tiled=True)
    return (later[None], present[None], model_grad)


def solution(mesh):
    in_specs = (
        P("shot", "blk", None, None),
        P("shot", "blk", None, None),
        P("shot", "blk", None, None),
        P("shot", "blk", None, None),
        P("blk", "shot", None),
        P("blk", "shot", None),
        P("blk", "shot", None),
        P("blk", "shot", None),
        P("shot"),
        P(),
        P("shot", None),
        P("shot", None, None),
        P("shot"),
        P("shot"),
        P("shot"),
        P("shot", None),
        P("shot", None),
        P("shot", None),
    )
    out_specs = (P("shot", "blk", None, None), P("shot", "blk", None, None), P("blk", "shot", None))
    return jax.shard_map(
        on_device, mesh=mesh, in_specs=in_specs, out_specs=out_specs, check_vma=False
    )
```

profile of v0, /device:TPU:56, one launch (start us, length us, event | category | flops | bytes accessed | tf_op | source)
XLA Modules:
  0.0 521.9 jit_solution(15416640213191718624)
XLA Ops:
  7.2 1.7 slice_bitcast_fusion.1
  8.9 1.9 collective-permute-start.17
  10.8 3.6 collective-permute-start.16
  15.1 51.3 %all_gather.13 = f32[8,128,128]{2,1,0:T(8,128)S(1)} all-gather(f32[8,8,128]{2,1,0:T(8,128)} %param.22), channel_id=1, replica_groups=mesh['shot'=16,'blk'=32] {'shot'}, dimensions={1}, use_global_device_ids=true | all-gather | bytes 557056 | tf_op jit(solution)/shard_map/all_gather | solution.py:85
  66.6 1.5 dynamic_update_slice.16
  68.9 1.9 collective-permute-start.1
  70.8 3.6 collective-permute-start
  74.5 43.0 %all_gather.12 = f32[8,128,128]{2,1,0:T(8,128)S(1)} all-gather(f32[8,8,128]{2,1,0:T(8,128)S(1)} %copy-done.14), channel_id=1, replica_groups=mesh['shot'=16,'blk'=32] {'shot'}, dimensions={1}, use_global_device_ids=true | all-gather | bytes 557056 | tf_op jit(solution)/shard_map/all_gather | solution.py:86
  117.5 44.4 %all_gather.14 = f32[8,128,128]{2,1,0:T(8,128)} all-gather(f32[8,8,128]{2,1,0:T(8,128)S(1)} %copy-done.15), channel_id=1, replica_groups=mesh['shot'=16,'blk'=32] {'shot'}, dimensions={1}, use_global_device_ids=true | all-gather | bytes 557056 | tf_op jit(solution)/shard_map/all_gather | solution.py:87
  161.9 43.6 %all_gather.15 = f32[8,128,128]{2,1,0:T(8,128)S(1)} all-gather(f32[8,8,128]{2,1,0:T(8,128)S(1)} %copy-done.16), channel_id=1, replica_groups=mesh['shot'=16,'blk'=32] {'shot'}, dimensions={1}, use_global_device_ids=true | all-gather | bytes 557056 | tf_op jit(solution)/shard_map/all_gather | solution.py:88
  207.5 1.4 fusion.700
  212.4 1.5 dynamic_update_slice.15
  214.0 2.8 dynamic_update_slice.17
  216.8 1.3 broadcast.105.clone.2
  218.1 3.5 dynamic_update_slice.18
  222.3 8.0 %multiply_subtract_fusion.9 = (f32[8,64,128]{2,1,0:T(8,128)S(1)}, f32[8,64,128]{2,1,0:T(8,128)S(1)}, f32[8,64,128]{2,1,0:T(8,128)S(1)}, f32[8,64,128]{2,1,0:T(8,...) fusion(f32[8,320,128]{2,1,0:T(8,128)S(1)} %dynamic_update_slice.15, ...), kind=kLoop, calls=%fused_computation.1159 | loop fusion | flops 3735552 | bytes 3145729 | tf_op jit(solution)/shard_map/sub | solution.py:49
  231.8 2.1 multiply_subtract_fusion.21
  234.2 2.1 collective-permute-start.3
  236.2 3.6 collective-permute-start.2
  239.9 16.8 %collective-permute-start.19 = (f32[4,64,128]{2,1,0:T(8,128)S(1)}, f32[4,64,128]{2,1,0:T(8,128)S(1)}, u32[]{:S(2)}, u32[]{:S(2)}) collective-permute-start(f32[4,64,128]{2,1,0:T(8,128)S(1)} %get-tuple-element.99), channel_id=1, source_target_pairs={{0,1},{1,2},{2,3},{3,4},{4,5},{5,6},{6,7},{7,8},{8,9},{9,10},{10,1... | collective-permute-start | bytes 393224 | tf_op jit(solution)/shard_map/ppermute | solution.py:17
  256.7 1.9 collective-permute-start.18
  259.4 9.7 %collective-permute-start.5 = (f32[4,64,128]{2,1,0:T(8,128)S(1)}, f32[4,64,128]{2,1,0:T(8,128)S(1)}, u32[]{:S(2)}, u32[]{:S(2)}) collective-permute-start(f32[4,64,128]{2,1,0:T(8,128)S(1)} %get-tuple-element.81), channel_id=1, source_target_pairs={{0,1},{1,2},{2,3},{3,4},{4,5},{5,6},{6,7},{7,8},{8,9},{9,10},{10,1... | collective-permute-start | bytes 393224 | tf_op jit(solution)/shard_map/ppermute | solution.py:17
  269.0 1.9 collective-permute-start.4
  272.3 7.3 %collective-permute-done.4 = f32[4,64,128]{2,1,0:T(8,128)S(1)} collective-permute-done((f32[4,64,128]{2,1,0:T(8,128)S(1)}, f32[4,64,128]{2,1,0:T(8,128)S(1)}, u32[]{:S(2)}, u32[]{:S(2)}) %collective-permute-start.4) | collective-permute-done | bytes 131104 | tf_op jit(solution)/shard_map/ppermute | solution.py:18
  279.5 2.1 multiply_subtract_fusion.18
  281.8 11.5 %collective-permute-start.7 = (f32[4,64,128]{2,1,0:T(8,128)S(1)}, f32[4,64,128]{2,1,0:T(8,128)S(1)}, u32[]{:S(2)}, u32[]{:S(2)}) collective-permute-start(f32[4,64,128]{2,1,0:T(8,128)S(1)} %get-tuple-element.79), channel_id=1, source_target_pairs={{0,1},{1,2},{2,3},{3,4},{4,5},{5,6},{6,7},{7,8},{8,9},{9,10},{10,1... | collective-permute-start | bytes 393224 | tf_op jit(solution)/shard_map/ppermute | solution.py:17
  293.2 1.9 collective-permute-start.6
  295.2 2.4 collective-permute-start.21
  297.6 3.2 collective-permute-start.20
  301.5 7.9 %collective-permute-start.9 = (f32[4,64,128]{2,1,0:T(8,128)S(1)}, f32[4,64,128]{2,1,0:T(8,128)S(1)}, u32[]{:S(2)}, u32[]{:S(2)}) collective-permute-start(f32[4,64,128]{2,1,0:T(8,128)S(1)} %get-tuple-element.77), channel_id=1, source_target_pairs={{0,1},{1,2},{2,3},{3,4},{4,5},{5,6},{6,7},{7,8},{8,9},{9,10},{10,1... | collective-permute-start | bytes 393224 | tf_op jit(solution)/shard_map/ppermute | solution.py:17
  309.4 2.1 collective-permute-start.8
  311.5 2.1 multiply_subtract_fusion.6
  313.7 6.3 %collective-permute-done.8 = f32[4,64,128]{2,1,0:T(8,128)S(1)} collective-permute-done((f32[4,64,128]{2,1,0:T(8,128)S(1)}, f32[4,64,128]{2,1,0:T(8,128)S(1)}, u32[]{:S(2)}, u32[]{:S(2)}) %collective-permute-start.8) | collective-permute-done | bytes 131104 | tf_op jit(solution)/shard_map/ppermute | solution.py:18
  319.9 2.0 multiply_subtract_fusion.15
  322.2 11.5 %collective-permute-start.23 = (f32[4,64,128]{2,1,0:T(8,128)S(1)}, f32[4,64,128]{2,1,0:T(8,128)S(1)}, u32[]{:S(2)}, u32[]{:S(2)}) collective-permute-start(f32[4,64,128]{2,1,0:T(8,128)S(1)} %get-tuple-element.95), channel_id=1, source_target_pairs={{0,1},{1,2},{2,3},{3,4},{4,5},{5,6},{6,7},{7,8},{8,9},{9,10},{10,1... | collective-permute-start | bytes 393224 | tf_op jit(solution)/shard_map/ppermute | solution.py:17
  333.7 1.9 collective-permute-start.22
  335.6 2.5 collective-permute-done.22
  338.1 1.3 select_add_fusion.1
  339.5 9.8 %collective-permute-start.25 = (f32[4,64,128]{2,1,0:T(8,128)S(1)}, f32[4,64,128]{2,1,0:T(8,128)S(1)}, u32[]{:S(2)}, u32[]{:S(2)}) collective-permute-start(f32[4,64,128]{2,1,0:T(8,128)S(1)} %get-tuple-element.93), channel_id=1, source_target_pairs={{0,1},{1,2},{2,3},{3,4},{4,5},{5,6},{6,7},{7,8},{8,9},{9,10},{10,1... | collective-permute-start | bytes 393224 | tf_op jit(solution)/shard_map/ppermute | solution.py:17
  349.3 1.9 collective-permute-start.24
  351.3 2.5 collective-permute-done.24
  353.7 2.1 multiply_subtract_fusion.3
  356.0 9.8 %collective-permute-start.27 = (f32[4,64,128]{2,1,0:T(8,128)S(1)}, f32[4,64,128]{2,1,0:T(8,128)S(1)}, u32[]{:S(2)}, u32[]{:S(2)}) collective-permute-start(f32[4,64,128]{2,1,0:T(8,128)S(1)} %get-tuple-element.91), channel_id=1, source_target_pairs={{0,1},{1,2},{2,3},{3,4},{4,5},{5,6},{6,7},{7,8},{8,9},{9,10},{10,1... | collective-permute-start | bytes 393224 | tf_op jit(solution)/shard_map/ppermute | solution.py:17
  365.8 1.9 collective-permute-start.26
  367.7 2.5 collective-permute-done.26
  370.2 1.4 select_add_fusion
  371.6 9.8 %collective-permute-start.29 = (f32[4,64,128]{2,1,0:T(8,128)S(1)}, f32[4,64,128]{2,1,0:T(8,128)S(1)}, u32[]{:S(2)}, u32[]{:S(2)}) collective-permute-start(f32[4,64,128]{2,1,0:T(8,128)S(1)} %get-tuple-element.89), channel_id=1, source_target_pairs={{0,1},{1,2},{2,3},{3,4},{4,5},{5,6},{6,7},{7,8},{8,9},{9,10},{10,1... | collective-permute-start | bytes 393224 | tf_op jit(solution)/shard_map/ppermute | solution.py:17
  381.4 1.9 collective-permute-start.28
  383.4 2.4 collective-permute-start.11
  385.8 3.2 collective-permute-start.10
  389.0 2.1 multiply_subtract_fusion
  391.2 7.9 %collective-permute-start.31 = (f32[4,64,128]{2,1,0:T(8,128)S(1)}, f32[4,64,128]{2,1,0:T(8,128)S(1)}, u32[]{:S(2)}, u32[]{:S(2)}) collective-permute-start(f32[4,64,128]{2,1,0:T(8,128)S(1)} %get-tuple-element.87), channel_id=1, source_target_pairs={{0,1},{1,2},{2,3},{3,4},{4,5},{5,6},{6,7},{7,8},{8,9},{9,10},{10,1... | collective-permute-start | bytes 393224 | tf_op jit(solution)/shard_map/ppermute | solution.py:17
  399.2 1.9 collective-permute-start.30
  401.5 8.2 %collective-permute-done.30 = f32[4,64,128]{2,1,0:T(8,128)S(1)} collective-permute-done((f32[4,64,128]{2,1,0:T(8,128)S(1)}, f32[4,64,128]{2,1,0:T(8,128)S(1)}, u32[]{:S(2)}, u32[]{:S(2)}) %collective-permute-start.30) | collective-permute-done | bytes 131104 | tf_op jit(solution)/shard_map/ppermute | solution.py:18
  409.7 2.7 fusion.198
  413.2 11.5 %collective-permute-start.13 = (f32[4,64,128]{2,1,0:T(8,128)}, f32[4,64,128]{2,1,0:T(8,128)S(1)}, u32[]{:S(2)}, u32[]{:S(2)}) collective-permute-start(f32[4,64,128]{2,1,0:T(8,128)} %get-tuple-element.73), channel_id=1, source_target_pairs={{0,1},{1,2},{2,3},{3,4},{4,5},{5,6},{6,7},{7,8},{8,9},{9,10},{10,1... | collective-permute-start | bytes 393224 | tf_op jit(solution)/shard_map/ppermute | solution.py:17
  424.6 1.9 collective-permute-start.12
  427.4 1.8 dynamic_update_slice.19
  429.4 2.9 multiply_subtract_fusion.12
  432.5 9.8 %collective-permute-start.15 = (f32[4,64,128]{2,1,0:T(8,128)S(1)}, f32[4,64,128]{2,1,0:T(8,128)S(1)}, u32[]{:S(2)}, u32[]{:S(2)}) collective-permute-start(f32[4,64,128]{2,1,0:T(8,128)S(1)} %get-tuple-element.71), channel_id=1, source_target_pairs={{0,1},{1,2},{2,3},{3,4},{4,5},{5,6},{6,7},{7,8},{8,9},{9,10},{10,1... | collective-permute-start | bytes 393224 | tf_op jit(solution)/shard_map/ppermute | solution.py:17
  442.3 1.9 collective-permute-start.14
  444.6 2.1 collective-permute-done.14
  446.7 1.3 fusion.98
  448.0 67.0 %reduce-scatter.2.cloned.1.call-done = f32[8,8,128]{2,1,0:T(8,128)} async-done(((f32[8,128,128]{2,1,0:T(8,128)}), f32[8,8,128]{2,1,0:T(8,128)}) %reduce-scatter.2.cloned.1.call-update) | async-done | bytes 32784 | tf_op jit(solution)/shard_map/reduce_scatter | solution.py:157
  (116 shorter events, 12.1 us)
Async XLA Ops:
  7.2 507.9 %reduce-scatter.2.cloned.1.call-start = ((), (), s32[]{:S(2)}) async-start(), calls=%async_computation.1 | async-start | bytes 557056 | tf_op jit(solution)/shard_map/reduce_scatter | solution.py:157
  8.9 213.4 %collective-permute-start.17 = (f32[4,64,128]{2,1,0:T(8,128)}, f32[4,64,128]{2,1,0:T(8,128)}, u32[]{:S(2)}, u32[]{:S(2)}) collective-permute-start(f32[4,64,128]{2,1,0:T(8,128)} %get-tuple-element.101), channel_id=1, source_target_pairs={{0,1},{1,2},{2,3},{3,4},{4,5},{5,6},{6,7},{7,8},{8,9},{9,10},{10,1... | collective-permute-start | bytes 393224 | tf_op jit(solution)/shard_map/ppermute | solution.py:17
  10.8 211.5 %collective-permute-start.16 = (f32[4,64,128]{2,1,0:T(8,128)}, f32[4,64,128]{2,1,0:T(8,128)}, u32[]{:S(2)}, u32[]{:S(2)}) collective-permute-start(f32[4,64,128]{2,1,0:T(8,128)} %get-tuple-element.100), channel_id=1, source_target_pairs={{1,0},{2,1},{3,2},{4,3},{5,4},{6,5},{7,6},{8,7},{9,8},{10,9},{11,1... | collective-permute-start | bytes 393224 | tf_op jit(solution)/shard_map/ppermute | solution.py:18
  66.5 1.6 copy-start.5
  66.6 7.9 %copy-start.14 = (f32[8,8,128]{2,1,0:T(8,128)S(1)}, f32[8,8,128]{2,1,0:T(8,128)}, u32[]{:S(2)}) copy-start(f32[8,8,128]{2,1,0:T(8,128)} %param.23) | copy-start | bytes 98308
  66.6 50.9 %copy-start.15 = (f32[8,8,128]{2,1,0:T(8,128)S(1)}, f32[8,8,128]{2,1,0:T(8,128)}, u32[]{:S(2)}) copy-start(f32[8,8,128]{2,1,0:T(8,128)} %param.24) | copy-start | bytes 98308
  68.1 137.4 %copy-start.2 = (f32[8,320,128]{2,1,0:T(8,128)}, f32[8,320,128]{2,1,0:T(8,128)S(1)}, u32[]{:S(2)}) copy-start(f32[8,320,128]{2,1,0:T(8,128)S(1)} %dynamic_update_slice.16) | copy-start | bytes 3932164
  68.1 93.8 %copy-start.16 = (f32[8,8,128]{2,1,0:T(8,128)S(1)}, f32[8,8,128]{2,1,0:T(8,128)}, u32[]{:S(2)}) copy-start(f32[8,8,128]{2,1,0:T(8,128)} %param.25) | copy-start | bytes 98308
  68.1 138.0 %copy-start.7 = (f32[8,64,128]{2,1,0:T(8,128)}, f32[8,64,128]{2,1,0:T(8,128)S(1)}, u32[]{:S(2)}) copy-start(f32[8,64,128]{2,1,0:T(8,128)S(1)} %bitcast_multiply_fusion) | copy-start | bytes 786436
  68.1 139.3 %copy-start.23 = (s32[1,128]{1,0:T(1,128)S(1)}, s32[1,128]{1,0:T(1,128)}, u32[]{:S(2)}) copy-start(s32[1,128]{1,0:T(1,128)} %param.33) | copy-start | bytes 1540
  68.1 139.3 %copy-start.22 = (s32[1,128]{1,0:T(1,128)S(1)}, s32[1,128]{1,0:T(1,128)}, u32[]{:S(2)}) copy-start(s32[1,128]{1,0:T(1,128)} %param.34) | copy-start | bytes 1540
  68.2 140.8 %copy-start.17 = (s32[1,128]{1,0:T(1,128)S(1)}, s32[1,128]{1,0:T(1,128)}, u32[]{:S(2)}) copy-start(s32[1,128]{1,0:T(1,128)} %param.35) | copy-start | bytes 1540
  68.9 161.6 %collective-permute-start.1 = (f32[4,64,128]{2,1,0:T(8,128)}, f32[4,64,128]{2,1,0:T(8,128)S(1)}, u32[]{:S(2)}, u32[]{:S(2)}) collective-permute-start(f32[4,64,128]{2,1,0:T(8,128)} %get-tuple-element.85), channel_id=1, source_target_pairs={{0,1},{1,2},{2,3},{3,4},{4,5},{5,6},{6,7},{7,8},{8,9},{9,10},{10,1... | collective-permute-start | bytes 393224 | tf_op jit(solution)/shard_map/ppermute | solution.py:17
  70.8 159.7 %collective-permute-start = (f32[4,64,128]{2,1,0:T(8,128)}, f32[4,64,128]{2,1,0:T(8,128)}, u32[]{:S(2)}, u32[]{:S(2)}) collective-permute-start(f32[4,64,128]{2,1,0:T(8,128)} %get-tuple-element.84), channel_id=1, source_target_pairs={{1,0},{2,1},{3,2},{4,3},{5,4},{6,5},{7,6},{8,7},{9,8},{10,9},{11,1... | collective-permute-start | bytes 393224 | tf_op jit(solution)/shard_map/ppermute | solution.py:18
  216.8 13.6 %copy-start = (f32[8,320,128]{2,1,0:T(8,128)}, f32[8,320,128]{2,1,0:T(8,128)S(1)}, u32[]{:S(2)}) copy-start(f32[8,320,128]{2,1,0:T(8,128)S(1)} %dynamic_update_slice.17) | copy-start | bytes 3932164
  216.8 4.9 copy-start.19
  230.4 1.0 copy-start.8
  230.4 1.4 copy-start.1
  233.9 24.7 %copy-start.3 = (f32[8,320,128]{2,1,0:T(8,128)S(1)}, f32[8,320,128]{2,1,0:T(8,128)}, u32[]{:S(2)}) copy-start(f32[8,320,128]{2,1,0:T(8,128)} %copy-done.2) | copy-start | bytes 3932164
  234.0 24.7 %copy-start.6 = (f32[1,8,64,128]{3,2,1,0:T(8,128)S(1)}, f32[1,8,64,128]{3,2,1,0:T(8,128)}, u32[]{:S(2)}) copy-start(f32[1,8,64,128]{3,2,1,0:T(8,128)} %param.21) | copy-start | bytes 786436
  234.0 24.7 %copy-start.11 = (f32[512,128]{1,0:T(8,128)S(1)}, f32[512,128]{1,0:T(8,128)}, u32[]{:S(2)}) copy-start(f32[512,128]{1,0:T(8,128)} %fusion.663) | copy-start | bytes 786436
  234.0 24.7 %copy-start.13 = (f32[1,8,64,128]{3,2,1,0:T(8,128)S(1)}, f32[1,8,64,128]{3,2,1,0:T(8,128)}, u32[]{:S(2)}) copy-start(f32[1,8,64,128]{3,2,1,0:T(8,128)} %param.20) | copy-start | bytes 786436
  234.2 24.5 %collective-permute-start.3 = (f32[4,64,128]{2,1,0:T(8,128)S(1)}, f32[4,64,128]{2,1,0:T(8,128)S(1)}, u32[]{:S(2)}, u32[]{:S(2)}) collective-permute-start(f32[4,64,128]{2,1,0:T(8,128)S(1)} %get-tuple-element.83), channel_id=1, source_target_pairs={{0,1},{1,2},{2,3},{3,4},{4,5},{5,6},{6,7},{7,8},{8,9},{9,10},{10,1... | collective-permute-start | bytes 393224 | tf_op jit(solution)/shard_map/ppermute | solution.py:17
  236.2 22.4 %collective-permute-start.2 = (f32[4,64,128]{2,1,0:T(8,128)S(1)}, f32[4,64,128]{2,1,0:T(8,128)S(1)}, u32[]{:S(2)}, u32[]{:S(2)}) collective-permute-start(f32[4,64,128]{2,1,0:T(8,128)S(1)} %get-tuple-element.82), channel_id=1, source_target_pairs={{1,0},{2,1},{3,2},{4,3},{5,4},{6,5},{7,6},{8,7},{9,8},{10,9},{11,1... | collective-permute-start | bytes 393224 | tf_op jit(solution)/shard_map/ppermute | solution.py:18
  239.9 31.1 %collective-permute-start.19 = (f32[4,64,128]{2,1,0:T(8,128)S(1)}, f32[4,64,128]{2,1,0:T(8,128)S(1)}, u32[]{:S(2)}, u32[]{:S(2)}) collective-permute-start(f32[4,64,128]{2,1,0:T(8,128)S(1)} %get-tuple-element.99), channel_id=1, source_target_pairs={{0,1},{1,2},{2,3},{3,4},{4,5},{5,6},{6,7},{7,8},{8,9},{9,10},{10,1... | collective-permute-start | bytes 393224 | tf_op jit(solution)/shard_map/ppermute | solution.py:17
  256.7 14.3 %collective-permute-start.18 = (f32[4,64,128]{2,1,0:T(8,128)S(1)}, f32[4,64,128]{2,1,0:T(8,128)S(1)}, u32[]{:S(2)}, u32[]{:S(2)}) collective-permute-start(f32[4,64,128]{2,1,0:T(8,128)S(1)} %get-tuple-element.98), channel_id=1, source_target_pairs={{1,0},{2,1},{3,2},{4,3},{5,4},{6,5},{7,6},{8,7},{9,8},{10,9},{11,1... | collective-permute-start | bytes 393224 | tf_op jit(solution)/shard_map/ppermute | solution.py:18
  258.7 12.3 %copy-start.4 = (f32[1,8,64,128]{3,2,1,0:T(8,128)S(1)}, f32[1,8,64,128]{3,2,1,0:T(8,128)}, u32[]{:S(2)}) copy-start(f32[1,8,64,128]{3,2,1,0:T(8,128)} %param.19) | copy-start | bytes 786436
  258.7 12.3 %copy-start.12 = (f32[1,8,64,128]{3,2,1,0:T(8,128)S(1)}, f32[1,8,64,128]{3,2,1,0:T(8,128)}, u32[]{:S(2)}) copy-start(f32[1,8,64,128]{3,2,1,0:T(8,128)} %param.18) | copy-start | bytes 786436
  258.7 12.3 %copy-start.18 = (pred[64]{0:T(512)(128)(4,1)S(1)}, pred[64]{0:T(512)(128)(4,1)}, u32[]{:S(2)}) copy-start(pred[64]{0:T(512)(128)(4,1)} %iota_compare_fusion.7) | copy-start | bytes 196
  259.4 12.9 %collective-permute-start.5 = (f32[4,64,128]{2,1,0:T(8,128)S(1)}, f32[4,64,128]{2,1,0:T(8,128)S(1)}, u32[]{:S(2)}, u32[]{:S(2)}) collective-permute-start(f32[4,64,128]{2,1,0:T(8,128)S(1)} %get-tuple-element.81), channel_id=1, source_target_pairs={{0,1},{1,2},{2,3},{3,4},{4,5},{5,6},{6,7},{7,8},{8,9},{9,10},{10,1... | collective-permute-start | bytes 393224 | tf_op jit(solution)/shard_map/ppermute | solution.py:17
  269.0 10.5 %collective-permute-start.4 = (f32[4,64,128]{2,1,0:T(8,128)S(1)}, f32[4,64,128]{2,1,0:T(8,128)S(1)}, u32[]{:S(2)}, u32[]{:S(2)}) collective-permute-start(f32[4,64,128]{2,1,0:T(8,128)S(1)} %get-tuple-element.80), channel_id=1, source_target_pairs={{1,0},{2,1},{3,2},{4,3},{5,4},{6,5},{7,6},{8,7},{9,8},{10,9},{11,1... | collective-permute-start | bytes 393224 | tf_op jit(solution)/shard_map/ppermute | solution.py:18
  281.6 19.2 %copy-start.10 = (f32[512,128]{1,0:T(8,128)S(1)}, f32[512,128]{1,0:T(8,128)}, u32[]{:S(2)}) copy-start(f32[512,128]{1,0:T(8,128)} %fusion.661) | copy-start | bytes 786436
  281.8 19.0 %collective-permute-start.7 = (f32[4,64,128]{2,1,0:T(8,128)S(1)}, f32[4,64,128]{2,1,0:T(8,128)S(1)}, u32[]{:S(2)}, u32[]{:S(2)}) collective-permute-start(f32[4,64,128]{2,1,0:T(8,128)S(1)} %get-tuple-element.79), channel_id=1, source_target_pairs={{0,1},{1,2},{2,3},{3,4},{4,5},{5,6},{6,7},{7,8},{8,9},{9,10},{10,1... | collective-permute-start | bytes 393224 | tf_op jit(solution)/shard_map/ppermute | solution.py:17
  293.2 7.5 %collective-permute-start.6 = (f32[4,64,128]{2,1,0:T(8,128)S(1)}, f32[4,64,128]{2,1,0:T(8,128)S(1)}, u32[]{:S(2)}, u32[]{:S(2)}) collective-permute-start(f32[4,64,128]{2,1,0:T(8,128)S(1)} %get-tuple-element.78), channel_id=1, source_target_pairs={{1,0},{2,1},{3,2},{4,3},{5,4},{6,5},{7,6},{8,7},{9,8},{10,9},{11,1... | collective-permute-start | bytes 393224 | tf_op jit(solution)/shard_map/ppermute | solution.py:18
  295.2 16.3 %collective-permute-start.21 = (f32[4,64,128]{2,1,0:T(8,128)S(1)}, f32[4,64,128]{2,1,0:T(8,128)S(1)}, u32[]{:S(2)}, u32[]{:S(2)}) collective-permute-start(f32[4,64,128]{2,1,0:T(8,128)S(1)} %get-tuple-element.97), channel_id=1, source_target_pairs={{0,1},{1,2},{2,3},{3,4},{4,5},{5,6},{6,7},{7,8},{8,9},{9,10},{10,1... | collective-permute-start | bytes 393224 | tf_op jit(solution)/shard_map/ppermute | solution.py:17
  297.6 13.9 %collective-permute-start.20 = (f32[4,64,128]{2,1,0:T(8,128)S(1)}, f32[4,64,128]{2,1,0:T(8,128)S(1)}, u32[]{:S(2)}, u32[]{:S(2)}) collective-permute-start(f32[4,64,128]{2,1,0:T(8,128)S(1)} %get-tuple-element.96), channel_id=1, source_target_pairs={{1,0},{2,1},{3,2},{4,3},{5,4},{6,5},{7,6},{8,7},{9,8},{10,9},{11,1... | collective-permute-start | bytes 393224 | tf_op jit(solution)/shard_map/ppermute | solution.py:18
  301.5 12.2 %collective-permute-start.9 = (f32[4,64,128]{2,1,0:T(8,128)S(1)}, f32[4,64,128]{2,1,0:T(8,128)S(1)}, u32[]{:S(2)}, u32[]{:S(2)}) collective-permute-start(f32[4,64,128]{2,1,0:T(8,128)S(1)} %get-tuple-element.77), channel_id=1, source_target_pairs={{0,1},{1,2},{2,3},{3,4},{4,5},{5,6},{6,7},{7,8},{8,9},{9,10},{10,1... | collective-permute-start | bytes 393224 | tf_op jit(solution)/shard_map/ppermute | solution.py:17
  309.4 10.5 %collective-permute-start.8 = (f32[4,64,128]{2,1,0:T(8,128)S(1)}, f32[4,64,128]{2,1,0:T(8,128)S(1)}, u32[]{:S(2)}, u32[]{:S(2)}) collective-permute-start(f32[4,64,128]{2,1,0:T(8,128)S(1)} %get-tuple-element.76), channel_id=1, source_target_pairs={{1,0},{2,1},{3,2},{4,3},{5,4},{6,5},{7,6},{8,7},{9,8},{10,9},{11,1... | collective-permute-start | bytes 393224 | tf_op jit(solution)/shard_map/ppermute | solution.py:18
  322.2 13.4 %collective-permute-start.23 = (f32[4,64,128]{2,1,0:T(8,128)S(1)}, f32[4,64,128]{2,1,0:T(8,128)S(1)}, u32[]{:S(2)}, u32[]{:S(2)}) collective-permute-start(f32[4,64,128]{2,1,0:T(8,128)S(1)} %get-tuple-element.95), channel_id=1, source_target_pairs={{0,1},{1,2},{2,3},{3,4},{4,5},{5,6},{6,7},{7,8},{8,9},{9,10},{10,1... | collective-permute-start | bytes 393224 | tf_op jit(solution)/shard_map/ppermute | solution.py:17
  333.7 4.4 collective-permute-start.22
  339.5 11.7 %collective-permute-start.25 = (f32[4,64,128]{2,1,0:T(8,128)S(1)}, f32[4,64,128]{2,1,0:T(8,128)S(1)}, u32[]{:S(2)}, u32[]{:S(2)}) collective-permute-start(f32[4,64,128]{2,1,0:T(8,128)S(1)} %get-tuple-element.93), channel_id=1, source_target_pairs={{0,1},{1,2},{2,3},{3,4},{4,5},{5,6},{6,7},{7,8},{8,9},{9,10},{10,1... | collective-permute-start | bytes 393224 | tf_op jit(solution)/shard_map/ppermute | solution.py:17
  349.3 4.4 collective-permute-start.24
  356.0 11.7 %collective-permute-start.27 = (f32[4,64,128]{2,1,0:T(8,128)S(1)}, f32[4,64,128]{2,1,0:T(8,128)S(1)}, u32[]{:S(2)}, u32[]{:S(2)}) collective-permute-start(f32[4,64,128]{2,1,0:T(8,128)S(1)} %get-tuple-element.91), channel_id=1, source_target_pairs={{0,1},{1,2},{2,3},{3,4},{4,5},{5,6},{6,7},{7,8},{8,9},{9,10},{10,1... | collective-permute-start | bytes 393224 | tf_op jit(solution)/shard_map/ppermute | solution.py:17
  365.8 4.4 collective-permute-start.26
  371.6 17.3 %collective-permute-start.29 = (f32[4,64,128]{2,1,0:T(8,128)S(1)}, f32[4,64,128]{2,1,0:T(8,128)S(1)}, u32[]{:S(2)}, u32[]{:S(2)}) collective-permute-start(f32[4,64,128]{2,1,0:T(8,128)S(1)} %get-tuple-element.89), channel_id=1, source_target_pairs={{0,1},{1,2},{2,3},{3,4},{4,5},{5,6},{6,7},{7,8},{8,9},{9,10},{10,1... | collective-permute-start | bytes 393224 | tf_op jit(solution)/shard_map/ppermute | solution.py:17
  381.4 7.5 %collective-permute-start.28 = (f32[4,64,128]{2,1,0:T(8,128)S(1)}, f32[4,64,128]{2,1,0:T(8,128)S(1)}, u32[]{:S(2)}, u32[]{:S(2)}) collective-permute-start(f32[4,64,128]{2,1,0:T(8,128)S(1)} %get-tuple-element.88), channel_id=1, source_target_pairs={{1,0},{2,1},{3,2},{4,3},{5,4},{6,5},{7,6},{8,7},{9,8},{10,9},{11,1... | collective-permute-start | bytes 393224 | tf_op jit(solution)/shard_map/ppermute | solution.py:18
  383.4 18.1 %collective-permute-start.11 = (f32[4,64,128]{2,1,0:T(8,128)S(1)}, f32[4,64,128]{2,1,0:T(8,128)S(1)}, u32[]{:S(2)}, u32[]{:S(2)}) collective-permute-start(f32[4,64,128]{2,1,0:T(8,128)S(1)} %get-tuple-element.75), channel_id=1, source_target_pairs={{0,1},{1,2},{2,3},{3,4},{4,5},{5,6},{6,7},{7,8},{8,9},{9,10},{10,1... | collective-permute-start | bytes 393224 | tf_op jit(solution)/shard_map/ppermute | solution.py:17
  385.8 15.7 %collective-permute-start.10 = (f32[4,64,128]{2,1,0:T(8,128)S(1)}, f32[4,64,128]{2,1,0:T(8,128)S(1)}, u32[]{:S(2)}, u32[]{:S(2)}) collective-permute-start(f32[4,64,128]{2,1,0:T(8,128)S(1)} %get-tuple-element.74), channel_id=1, source_target_pairs={{1,0},{2,1},{3,2},{4,3},{5,4},{6,5},{7,6},{8,7},{9,8},{10,9},{11,1... | collective-permute-start | bytes 393224 | tf_op jit(solution)/shard_map/ppermute | solution.py:18
  391.0 10.1 %copy-start.21 = (f32[128]{0:T(128)S(1)}, f32[128]{0:T(128)}, u32[]{:S(2)}) copy-start(f32[128]{0:T(128)} %get-tuple-element.105) | copy-start | bytes 1540
  391.2 10.3 %collective-permute-start.31 = (f32[4,64,128]{2,1,0:T(8,128)S(1)}, f32[4,64,128]{2,1,0:T(8,128)S(1)}, u32[]{:S(2)}, u32[]{:S(2)}) collective-permute-start(f32[4,64,128]{2,1,0:T(8,128)S(1)} %get-tuple-element.87), channel_id=1, source_target_pairs={{0,1},{1,2},{2,3},{3,4},{4,5},{5,6},{6,7},{7,8},{8,9},{9,10},{10,1... | collective-permute-start | bytes 393224 | tf_op jit(solution)/shard_map/ppermute | solution.py:17
  399.2 10.5 %collective-permute-start.30 = (f32[4,64,128]{2,1,0:T(8,128)S(1)}, f32[4,64,128]{2,1,0:T(8,128)S(1)}, u32[]{:S(2)}, u32[]{:S(2)}) collective-permute-start(f32[4,64,128]{2,1,0:T(8,128)S(1)} %get-tuple-element.86), channel_id=1, source_target_pairs={{1,0},{2,1},{3,2},{4,3},{5,4},{6,5},{7,6},{8,7},{9,8},{10,9},{11,1... | collective-permute-start | bytes 393224 | tf_op jit(solution)/shard_map/ppermute | solution.py:18
  412.4 34.3 %copy-start.9 = (f32[8,64,128]{2,1,0:T(8,128)}, f32[8,64,128]{2,1,0:T(8,128)S(1)}, u32[]{:S(2)}) copy-start(f32[8,64,128]{2,1,0:T(8,128)S(1)} %get-tuple-element.4) | copy-start | bytes 786436
  413.2 16.1 %collective-permute-start.13 = (f32[4,64,128]{2,1,0:T(8,128)}, f32[4,64,128]{2,1,0:T(8,128)S(1)}, u32[]{:S(2)}, u32[]{:S(2)}) collective-permute-start(f32[4,64,128]{2,1,0:T(8,128)} %get-tuple-element.73), channel_id=1, source_target_pairs={{0,1},{1,2},{2,3},{3,4},{4,5},{5,6},{6,7},{7,8},{8,9},{9,10},{10,1... | collective-permute-start | bytes 393224 | tf_op jit(solution)/shard_map/ppermute | solution.py:17
  424.6 4.7 collective-permute-start.12
  432.3 11.9 %copy-start.20 = (f32[128]{0:T(128)S(1)}, f32[128]{0:T(128)}, u32[]{:S(2)}) copy-start(f32[128]{0:T(128)} %get-tuple-element.102) | copy-start | bytes 1540
  432.5 12.1 %collective-permute-start.15 = (f32[4,64,128]{2,1,0:T(8,128)S(1)}, f32[4,64,128]{2,1,0:T(8,128)S(1)}, u32[]{:S(2)}, u32[]{:S(2)}) collective-permute-start(f32[4,64,128]{2,1,0:T(8,128)S(1)} %get-tuple-element.71), channel_id=1, source_target_pairs={{0,1},{1,2},{2,3},{3,4},{4,5},{5,6},{6,7},{7,8},{8,9},{9,10},{10,1... | collective-permute-start | bytes 393224 | tf_op jit(solution)/shard_map/ppermute | solution.py:17
  442.3 4.4 collective-permute-start.14
Sparse Core Ops, SparseCore 0:
  429.4 85.6 reduce-scatter.1
where the time goes:
time: 523 us; the launch traced here: 522 us
  blocking collectives  182 us (35%)
  starting transfers between devices  165 us (32%)
  waiting for transfers between devices  98.5 us (19%)
  other arithmetic  34.3 us (7%)
  local copies, waits for them, and re-layouts  20.4 us (4%)
  between operations  18.4 us (4%)
    ppermute x16, starting transfers between devices, padded_2(): before = lax.ppermute(last, axis, up)  127 us
    reduce_scatter x1, waiting for transfers between devices, on_device(): lax.psum_scatter(grad_slab, 'shot', scatter_dimension=1, tiled=True)  67 us
    all_gather x1, blocking collectives, on_device(): lax.all_gather(courant_sq, 'shot', axis=1, tiled=True)  51.3 us
    all_gather x1, blocking collectives, on_device(): lax.all_gather(tilt_angle, 'shot', axis=1, tiled=True)  44.4 us
    all_gather x1, blocking collectives, on_device(): lax.all_gather(azimuth, 'shot', axis=1, tiled=True)  43.6 us
    all_gather x1, blocking collectives, on_device(): lax.all_gather(epsilon, 'shot', axis=1, tiled=True)  43 us
    ppermute x16, starting transfers between devices, padded_2(): after = lax.ppermute(leading, axis, down)  38.5 us
    ppermute x16, waiting for transfers between devices, padded_2(): after = lax.ppermute(leading, axis, down)  31.4 us
  transfers between devices with their start and end apart: 33, of which 9 were waited for; matrix products, arithmetic and copies ran while one was open for 8% of the time, Pallas kernels for 0%

commit v1 on v0

--- a/solution.py
+++ b/solution.py
@@ -84,7 +84,9 @@
     pieces = (
         lax.all_gather(courant_sq, "shot", axis=1, tiled=True),
         lax.all_gather(epsilon, "shot", axis=1, tiled=True),
-        lax.all_gather(tilt_angle, "shot", axis=1, tiled=True),
+        jnp.concatenate(
+            lax.all_to_all(jnp.stack([tilt_angle] * lax.axis_size("shot")), "shot", 0, 0), axis=1
+        ),
         lax.all_gather(azimuth, "shot", axis=1, tiled=True),
     )
     count = pieces[0].shape[1]

time: 523 us -> 488 us (0.933)
  blocking collectives: 182 us -> 136 us
  starting transfers between devices: 165 us -> 176 us
    all_gather x1 -> x0, blocking collectives: 44.4 us -> none  [on_device(): lax.all_gather(tilt_angle, 'shot', axis=1, tiled=True)]
    all_to_all x0 -> x1, starting transfers between devices: none -> 9.83 us  [on_device(): lax.all_to_all(jnp.stack([tilt_angle] * lax.axis_size('shot')), 'shot', 0...]
  transfers between devices with their start and end apart: 33 -> 34, of which waited for: 9 -> 9; matrix products, arithmetic and copies ran while one was open for 8% -> 8% of each run, Pallas kernels for 0% -> 0%
where the time goes in v1:
time: 488 us; the launch traced here: 487 us
  starting transfers between devices  176 us (36%)
  blocking collectives  136 us (28%)
  waiting for transfers between devices  98.5 us (20%)
  other arithmetic  30.4 us (6%)
  local copies, waits for them, and re-layouts  24 us (5%)
  between operations  18.4 us (4%)
    ppermute x16, starting transfers between devices, padded_2(): before = lax.ppermute(last, axis, up)  128 us
    reduce_scatter x1, waiting for transfers between devices, on_device(): lax.psum_scatter(grad_slab, 'shot', scatter_dimension=1, tiled=True)  67 us
    all_gather x1, blocking collectives, on_device(): lax.all_gather(courant_sq, 'shot', axis=1, tiled=True)  49.3 us
    all_gather x1, blocking collectives, on_device(): lax.all_gather(epsilon, 'shot', axis=1, tiled=True)  44.2 us
    all_gather x1, blocking collectives, on_device(): lax.all_gather(azimuth, 'shot', axis=1, tiled=True)  42.8 us
    ppermute x16, starting transfers between devices, padded_2(): after = lax.ppermute(leading, axis, down)  38.5 us
    ppermute x16, waiting for transfers between devices, padded_2(): after = lax.ppermute(leading, axis, down)  31.4 us
    sub x8, other arithmetic, operate_shallow(): flux_z = (1.0 + twice_eps) * slope_z - twice_eps * normal_z * normal_slope  19.6 us
  transfers between devices with their start and end apart: 34, of which 9 were waited for; matrix products, arithmetic and copies ran while one was open for 8% of the time, Pallas kernels for 0%

profile of v1, /device:TPU:56, one launch (start us, length us, event | category | flops | bytes accessed | tf_op | source)
XLA Modules:
  0.0 486.6 jit_solution(7245020446904782055)
XLA Ops:
  7.2 1.7 stack.2
  8.8 9.8 %all-to-all-start = ((f32[16,8,8,128]{3,2,1,0:T(8,128)}), f32[16,8,8,128]{3,2,1,0:T(8,128)S(1)}, u32[]{:S(2)}, u32[]{:S(2)}) async-start(f32[16,8,8,128]{3,2,1,0:T(8,128)} %stack.2), calls=%async_computation | async-start | bytes 1048576 | tf_op jit(solution)/shard_map/all_to_all | solution.py:88
  19.5 1.9 collective-permute-start.17
  21.4 3.6 collective-permute-start.16
  25.7 49.3 %all_gather.10 = f32[8,128,128]{2,1,0:T(8,128)S(1)} all-gather(f32[8,8,128]{2,1,0:T(8,128)S(1)} %copy-done.13), channel_id=1, replica_groups=mesh['shot'=16,'blk'=32] {'shot'}, dimensions={1}, use_global_device_ids=true | all-gather | bytes 557056 | tf_op jit(solution)/shard_map/all_gather | solution.py:85
  75.1 1.5 dynamic_update_slice.16
  77.5 1.9 collective-permute-start.1
  79.4 3.6 collective-permute-start
  84.4 1.4 fusion.700
  88.6 44.2 %all_gather.9 = f32[8,128,128]{2,1,0:T(8,128)} all-gather(f32[8,8,128]{2,1,0:T(8,128)S(1)} %copy-done.14), channel_id=1, replica_groups=mesh['shot'=16,'blk'=32] {'shot'}, dimensions={1}, use_global_device_ids=true | all-gather | bytes 557056 | tf_op jit(solution)/shard_map/all_gather | solution.py:86
  132.7 42.8 %all_gather.11 = f32[8,128,128]{2,1,0:T(8,128)S(1)} all-gather(f32[8,8,128]{2,1,0:T(8,128)S(1)} %copy-done.15), channel_id=1, replica_groups=mesh['shot'=16,'blk'=32] {'shot'}, dimensions={1}, use_global_device_ids=true | all-gather | bytes 557056 | tf_op jit(solution)/shard_map/all_gather | solution.py:90
  176.9 2.8 dynamic_update_slice.15
  180.9 3.5 dynamic_update_slice.18
  186.5 2.8 dynamic_update_slice.17
  190.4 4.3 multiply_subtract_fusion.9
  196.0 2.1 multiply_subtract_fusion.21
  198.3 2.1 collective-permute-start.3
  200.4 3.6 collective-permute-start.2
  204.1 18.0 %collective-permute-start.19 = (f32[4,64,128]{2,1,0:T(8,128)S(1)}, f32[4,64,128]{2,1,0:T(8,128)S(1)}, u32[]{:S(2)}, u32[]{:S(2)}) collective-permute-start(f32[4,64,128]{2,1,0:T(8,128)S(1)} %get-tuple-element.99), channel_id=1, source_target_pairs={{0,1},{1,2},{2,3},{3,4},{4,5},{5,6},{6,7},{7,8},{8,9},{9,10},{10,1... | collective-permute-start | bytes 393224 | tf_op jit(solution)/shard_map/ppermute | solution.py:17
  222.1 1.9 collective-permute-start.18
  224.8 9.7 %collective-permute-start.5 = (f32[4,64,128]{2,1,0:T(8,128)S(1)}, f32[4,64,128]{2,1,0:T(8,128)S(1)}, u32[]{:S(2)}, u32[]{:S(2)}) collective-permute-start(f32[4,64,128]{2,1,0:T(8,128)S(1)} %get-tuple-element.81), channel_id=1, source_target_pairs={{0,1},{1,2},{2,3},{3,4},{4,5},{5,6},{6,7},{7,8},{8,9},{9,10},{10,1... | collective-permute-start | bytes 393224 | tf_op jit(solution)/shard_map/ppermute | solution.py:17
  234.4 1.9 collective-permute-start.4
  236.4 1.4 fusion.655
  237.8 7.1 %collective-permute-done.4 = f32[4,64,128]{2,1,0:T(8,128)S(1)} collective-permute-done((f32[4,64,128]{2,1,0:T(8,128)S(1)}, f32[4,64,128]{2,1,0:T(8,128)S(1)}, u32[]{:S(2)}, u32[]{:S(2)}) %collective-permute-start.4) | collective-permute-done | bytes 131104 | tf_op jit(solution)/shard_map/ppermute | solution.py:18
  244.9 2.1 multiply_subtract_fusion.18
  247.2 11.5 %collective-permute-start.7 = (f32[4,64,128]{2,1,0:T(8,128)S(1)}, f32[4,64,128]{2,1,0:T(8,128)S(1)}, u32[]{:S(2)}, u32[]{:S(2)}) collective-permute-start(f32[4,64,128]{2,1,0:T(8,128)S(1)} %get-tuple-element.79), channel_id=1, source_target_pairs={{0,1},{1,2},{2,3},{3,4},{4,5},{5,6},{6,7},{7,8},{8,9},{9,10},{10,1... | collective-permute-start | bytes 393224 | tf_op jit(solution)/shard_map/ppermute | solution.py:17
  258.6 1.9 collective-permute-start.6
  260.6 2.4 collective-permute-start.21
  263.0 3.2 collective-permute-start.20
  266.9 7.9 %collective-permute-start.9 = (f32[4,64,128]{2,1,0:T(8,128)S(1)}, f32[4,64,128]{2,1,0:T(8,128)S(1)}, u32[]{:S(2)}, u32[]{:S(2)}) collective-permute-start(f32[4,64,128]{2,1,0:T(8,128)S(1)} %get-tuple-element.77), channel_id=1, source_target_pairs={{0,1},{1,2},{2,3},{3,4},{4,5},{5,6},{6,7},{7,8},{8,9},{9,10},{10,1... | collective-permute-start | bytes 393224 | tf_op jit(solution)/shard_map/ppermute | solution.py:17
  274.8 2.1 collective-permute-start.8
  277.0 2.1 multiply_subtract_fusion.6
  279.1 6.3 %collective-permute-done.8 = f32[4,64,128]{2,1,0:T(8,128)S(1)} collective-permute-done((f32[4,64,128]{2,1,0:T(8,128)S(1)}, f32[4,64,128]{2,1,0:T(8,128)S(1)}, u32[]{:S(2)}, u32[]{:S(2)}) %collective-permute-start.8) | collective-permute-done | bytes 131104 | tf_op jit(solution)/shard_map/ppermute | solution.py:18
  285.3 2.1 multiply_subtract_fusion.15
  287.6 11.5 %collective-permute-start.23 = (f32[4,64,128]{2,1,0:T(8,128)S(1)}, f32[4,64,128]{2,1,0:T(8,128)S(1)}, u32[]{:S(2)}, u32[]{:S(2)}) collective-permute-start(f32[4,64,128]{2,1,0:T(8,128)S(1)} %get-tuple-element.95), channel_id=1, source_target_pairs={{0,1},{1,2},{2,3},{3,4},{4,5},{5,6},{6,7},{7,8},{8,9},{9,10},{10,1... | collective-permute-start | bytes 393224 | tf_op jit(solution)/shard_map/ppermute | solution.py:17
  299.1 1.9 collective-permute-start.22
  301.1 2.5 collective-permute-done.22
  303.5 1.2 select_add_fusion.1
  304.8 9.8 %collective-permute-start.25 = (f32[4,64,128]{2,1,0:T(8,128)S(1)}, f32[4,64,128]{2,1,0:T(8,128)S(1)}, u32[]{:S(2)}, u32[]{:S(2)}) collective-permute-start(f32[4,64,128]{2,1,0:T(8,128)S(1)} %get-tuple-element.93), channel_id=1, source_target_pairs={{0,1},{1,2},{2,3},{3,4},{4,5},{5,6},{6,7},{7,8},{8,9},{9,10},{10,1... | collective-permute-start | bytes 393224 | tf_op jit(solution)/shard_map/ppermute | solution.py:17
  314.6 1.9 collective-permute-start.24
  316.6 2.5 collective-permute-done.24
  319.0 2.1 multiply_subtract_fusion.3
  321.3 9.8 %collective-permute-start.27 = (f32[4,64,128]{2,1,0:T(8,128)S(1)}, f32[4,64,128]{2,1,0:T(8,128)S(1)}, u32[]{:S(2)}, u32[]{:S(2)}) collective-permute-start(f32[4,64,128]{2,1,0:T(8,128)S(1)} %get-tuple-element.91), channel_id=1, source_target_pairs={{0,1},{1,2},{2,3},{3,4},{4,5},{5,6},{6,7},{7,8},{8,9},{9,10},{10,1... | collective-permute-start | bytes 393224 | tf_op jit(solution)/shard_map/ppermute | solution.py:17
  331.1 1.9 collective-permute-start.26
  333.0 2.5 collective-permute-done.26
  335.5 1.3 select_add_fusion
  336.8 9.8 %collective-permute-start.29 = (f32[4,64,128]{2,1,0:T(8,128)S(1)}, f32[4,64,128]{2,1,0:T(8,128)S(1)}, u32[]{:S(2)}, u32[]{:S(2)}) collective-permute-start(f32[4,64,128]{2,1,0:T(8,128)S(1)} %get-tuple-element.89), channel_id=1, source_target_pairs={{0,1},{1,2},{2,3},{3,4},{4,5},{5,6},{6,7},{7,8},{8,9},{9,10},{10,1... | collective-permute-start | bytes 393224 | tf_op jit(solution)/shard_map/ppermute | solution.py:17
  346.6 1.9 collective-permute-start.28
  348.6 2.4 collective-permute-start.11
  351.0 3.2 collective-permute-start.10
  354.2 2.1 multiply_subtract_fusion
  356.4 7.9 %collective-permute-start.31 = (f32[4,64,128]{2,1,0:T(8,128)S(1)}, f32[4,64,128]{2,1,0:T(8,128)S(1)}, u32[]{:S(2)}, u32[]{:S(2)}) collective-permute-start(f32[4,64,128]{2,1,0:T(8,128)S(1)} %get-tuple-element.87), channel_id=1, source_target_pairs={{0,1},{1,2},{2,3},{3,4},{4,5},{5,6},{6,7},{7,8},{8,9},{9,10},{10,1... | collective-permute-start | bytes 393224 | tf_op jit(solution)/shard_map/ppermute | solution.py:17
  364.4 1.9 collective-permute-start.30
  366.7 8.2 %collective-permute-done.30 = f32[4,64,128]{2,1,0:T(8,128)S(1)} collective-permute-done((f32[4,64,128]{2,1,0:T(8,128)S(1)}, f32[4,64,128]{2,1,0:T(8,128)S(1)}, u32[]{:S(2)}, u32[]{:S(2)}) %collective-permute-start.30) | collective-permute-done | bytes 131104 | tf_op jit(solution)/shard_map/ppermute | solution.py:18
  374.9 2.1 fusion.198
  377.8 11.5 %collective-permute-start.13 = (f32[4,64,128]{2,1,0:T(8,128)}, f32[4,64,128]{2,1,0:T(8,128)S(1)}, u32[]{:S(2)}, u32[]{:S(2)}) collective-permute-start(f32[4,64,128]{2,1,0:T(8,128)} %get-tuple-element.73), channel_id=1, source_target_pairs={{0,1},{1,2},{2,3},{3,4},{4,5},{5,6},{6,7},{7,8},{8,9},{9,10},{10,1... | collective-permute-start | bytes 393224 | tf_op jit(solution)/shard_map/ppermute | solution.py:17
  389.2 1.9 collective-permute-start.12
  392.0 1.7 dynamic_update_slice.19
  394.0 2.9 multiply_subtract_fusion.12
  397.1 9.8 %collective-permute-start.15 = (f32[4,64,128]{2,1,0:T(8,128)S(1)}, f32[4,64,128]{2,1,0:T(8,128)S(1)}, u32[]{:S(2)}, u32[]{:S(2)}) collective-permute-start(f32[4,64,128]{2,1,0:T(8,128)S(1)} %get-tuple-element.71), channel_id=1, source_target_pairs={{0,1},{1,2},{2,3},{3,4},{4,5},{5,6},{6,7},{7,8},{8,9},{9,10},{10,1... | collective-permute-start | bytes 393224 | tf_op jit(solution)/shard_map/ppermute | solution.py:17
  406.9 1.9 collective-permute-start.14
  409.2 2.1 collective-permute-done.14
  411.3 1.3 fusion.98
  412.7 67.0 %reduce-scatter.2.cloned.1.call-done = f32[8,8,128]{2,1,0:T(8,128)} async-done(((f32[8,128,128]{2,1,0:T(8,128)}), f32[8,8,128]{2,1,0:T(8,128)}) %reduce-scatter.2.cloned.1.call-update) | async-done | bytes 32784 | tf_op jit(solution)/shard_map/reduce_scatter | solution.py:159
  (119 shorter events, 15.2 us)
Async XLA Ops:
  7.2 11.6 %copy-start.4 = (f32[1,8,64,128]{3,2,1,0:T(8,128)S(1)}, f32[1,8,64,128]{3,2,1,0:T(8,128)}, u32[]{:S(2)}) copy-start(f32[1,8,64,128]{3,2,1,0:T(8,128)} %param.19) | copy-start | bytes 786436
  7.2 18.5 %copy-start.13 = (f32[8,8,128]{2,1,0:T(8,128)S(1)}, f32[8,8,128]{2,1,0:T(8,128)}, u32[]{:S(2)}) copy-start(f32[8,8,128]{2,1,0:T(8,128)} %param.22) | copy-start | bytes 98308
  8.8 176.8 %all-to-all-start = ((f32[16,8,8,128]{3,2,1,0:T(8,128)}), f32[16,8,8,128]{3,2,1,0:T(8,128)S(1)}, u32[]{:S(2)}, u32[]{:S(2)}) async-start(f32[16,8,8,128]{3,2,1,0:T(8,128)} %stack.2), calls=%async_computation | async-start | bytes 1048576 | tf_op jit(solution)/shard_map/all_to_all | solution.py:88
  18.7 461.1 %reduce-scatter.2.cloned.1.call-start = ((), (), s32[]{:S(2)}) async-start(), calls=%async_computation.2 | async-start | bytes 557056 | tf_op jit(solution)/shard_map/reduce_scatter | solution.py:159
  19.5 169.9 %collective-permute-start.17 = (f32[4,64,128]{2,1,0:T(8,128)}, f32[4,64,128]{2,1,0:T(8,128)}, u32[]{:S(2)}, u32[]{:S(2)}) collective-permute-start(f32[4,64,128]{2,1,0:T(8,128)} %get-tuple-element.101), channel_id=1, source_target_pairs={{0,1},{1,2},{2,3},{3,4},{4,5},{5,6},{6,7},{7,8},{8,9},{9,10},{10,1... | collective-permute-start | bytes 393224 | tf_op jit(solution)/shard_map/ppermute | solution.py:17
  21.4 168.0 %collective-permute-start.16 = (f32[4,64,128]{2,1,0:T(8,128)}, f32[4,64,128]{2,1,0:T(8,128)}, u32[]{:S(2)}, u32[]{:S(2)}) collective-permute-start(f32[4,64,128]{2,1,0:T(8,128)} %get-tuple-element.100), channel_id=1, source_target_pairs={{1,0},{2,1},{3,2},{4,3},{5,4},{6,5},{7,6},{8,7},{9,8},{10,9},{11,1... | collective-permute-start | bytes 393224 | tf_op jit(solution)/shard_map/ppermute | solution.py:18
  75.0 1.6 copy-start.5
  75.1 9.3 %copy-start.23 = (s32[1,128]{1,0:T(1,128)S(1)}, s32[1,128]{1,0:T(1,128)}, u32[]{:S(2)}) copy-start(s32[1,128]{1,0:T(1,128)} %param.33) | copy-start | bytes 1540
  75.1 9.3 %copy-start.22 = (s32[1,128]{1,0:T(1,128)S(1)}, s32[1,128]{1,0:T(1,128)}, u32[]{:S(2)}) copy-start(s32[1,128]{1,0:T(1,128)} %param.34) | copy-start | bytes 1540
  75.1 10.7 %copy-start.16 = (s32[1,128]{1,0:T(1,128)S(1)}, s32[1,128]{1,0:T(1,128)}, u32[]{:S(2)}) copy-start(s32[1,128]{1,0:T(1,128)} %param.35) | copy-start | bytes 1540
  75.1 13.5 %copy-start.14 = (f32[8,8,128]{2,1,0:T(8,128)S(1)}, f32[8,8,128]{2,1,0:T(8,128)}, u32[]{:S(2)}) copy-start(f32[8,8,128]{2,1,0:T(8,128)} %param.23) | copy-start | bytes 98308
  76.6 99.0 %copy-start.2 = (f32[8,320,128]{2,1,0:T(8,128)}, f32[8,320,128]{2,1,0:T(8,128)S(1)}, u32[]{:S(2)}) copy-start(f32[8,320,128]{2,1,0:T(8,128)S(1)} %dynamic_update_slice.16) | copy-start | bytes 3932164
  76.6 56.1 %copy-start.15 = (f32[8,8,128]{2,1,0:T(8,128)S(1)}, f32[8,8,128]{2,1,0:T(8,128)}, u32[]{:S(2)}) copy-start(f32[8,8,128]{2,1,0:T(8,128)} %param.25) | copy-start | bytes 98308
  77.5 117.3 %collective-permute-start.1 = (f32[4,64,128]{2,1,0:T(8,128)}, f32[4,64,128]{2,1,0:T(8,128)S(1)}, u32[]{:S(2)}, u32[]{:S(2)}) collective-permute-start(f32[4,64,128]{2,1,0:T(8,128)} %get-tuple-element.85), channel_id=1, source_target_pairs={{0,1},{1,2},{2,3},{3,4},{4,5},{5,6},{6,7},{7,8},{8,9},{9,10},{10,1... | collective-permute-start | bytes 393224 | tf_op jit(solution)/shard_map/ppermute | solution.py:17
  79.4 115.4 %collective-permute-start = (f32[4,64,128]{2,1,0:T(8,128)}, f32[4,64,128]{2,1,0:T(8,128)}, u32[]{:S(2)}, u32[]{:S(2)}) collective-permute-start(f32[4,64,128]{2,1,0:T(8,128)} %get-tuple-element.84), channel_id=1, source_target_pairs={{1,0},{2,1},{3,2},{4,3},{5,4},{6,5},{7,6},{8,7},{9,8},{10,9},{11,1... | collective-permute-start | bytes 393224 | tf_op jit(solution)/shard_map/ppermute | solution.py:18
  179.7 4.7 copy-start.19
  189.3 1.1 copy-start
  194.7 1.3 copy-start.1
  198.1 25.9 %copy-start.3 = (f32[8,320,128]{2,1,0:T(8,128)S(1)}, f32[8,320,128]{2,1,0:T(8,128)}, u32[]{:S(2)}) copy-start(f32[8,320,128]{2,1,0:T(8,128)} %copy-done.2) | copy-start | bytes 3932164
  198.1 25.9 %copy-start.10 = (f32[512,128]{1,0:T(8,128)S(1)}, f32[512,128]{1,0:T(8,128)}, u32[]{:S(2)}) copy-start(f32[512,128]{1,0:T(8,128)} %fusion.663) | copy-start | bytes 786436
  198.1 25.9 %copy-start.12 = (f32[1,8,64,128]{3,2,1,0:T(8,128)S(1)}, f32[1,8,64,128]{3,2,1,0:T(8,128)}, u32[]{:S(2)}) copy-start(f32[1,8,64,128]{3,2,1,0:T(8,128)} %param.20) | copy-start | bytes 786436
  198.3 25.7 %collective-permute-start.3 = (f32[4,64,128]{2,1,0:T(8,128)S(1)}, f32[4,64,128]{2,1,0:T(8,128)S(1)}, u32[]{:S(2)}, u32[]{:S(2)}) collective-permute-start(f32[4,64,128]{2,1,0:T(8,128)S(1)} %get-tuple-element.83), channel_id=1, source_target_pairs={{0,1},{1,2},{2,3},{3,4},{4,5},{5,6},{6,7},{7,8},{8,9},{9,10},{10,1... | collective-permute-start | bytes 393224 | tf_op jit(solution)/shard_map/ppermute | solution.py:17
  200.4 23.7 %collective-permute-start.2 = (f32[4,64,128]{2,1,0:T(8,128)S(1)}, f32[4,64,128]{2,1,0:T(8,128)S(1)}, u32[]{:S(2)}, u32[]{:S(2)}) collective-permute-start(f32[4,64,128]{2,1,0:T(8,128)S(1)} %get-tuple-element.82), channel_id=1, source_target_pairs={{1,0},{2,1},{3,2},{4,3},{5,4},{6,5},{7,6},{8,7},{9,8},{10,9},{11,1... | collective-permute-start | bytes 393224 | tf_op jit(solution)/shard_map/ppermute | solution.py:18
  204.1 32.3 %collective-permute-start.19 = (f32[4,64,128]{2,1,0:T(8,128)S(1)}, f32[4,64,128]{2,1,0:T(8,128)S(1)}, u32[]{:S(2)}, u32[]{:S(2)}) collective-permute-start(f32[4,64,128]{2,1,0:T(8,128)S(1)} %get-tuple-element.99), channel_id=1, source_target_pairs={{0,1},{1,2},{2,3},{3,4},{4,5},{5,6},{6,7},{7,8},{8,9},{9,10},{10,1... | collective-permute-start | bytes 393224 | tf_op jit(solution)/shard_map/ppermute | solution.py:17
  222.1 14.3 %collective-permute-start.18 = (f32[4,64,128]{2,1,0:T(8,128)S(1)}, f32[4,64,128]{2,1,0:T(8,128)S(1)}, u32[]{:S(2)}, u32[]{:S(2)}) collective-permute-start(f32[4,64,128]{2,1,0:T(8,128)S(1)} %get-tuple-element.98), channel_id=1, source_target_pairs={{1,0},{2,1},{3,2},{4,3},{5,4},{6,5},{7,6},{8,7},{9,8},{10,9},{11,1... | collective-permute-start | bytes 393224 | tf_op jit(solution)/shard_map/ppermute | solution.py:18
  224.1 12.3 %copy-start.11 = (f32[1,8,64,128]{3,2,1,0:T(8,128)S(1)}, f32[1,8,64,128]{3,2,1,0:T(8,128)}, u32[]{:S(2)}) copy-start(f32[1,8,64,128]{3,2,1,0:T(8,128)} %param.18) | copy-start | bytes 786436
  224.1 12.3 %copy-start.17 = (pred[64]{0:T(512)(128)(4,1)S(1)}, pred[64]{0:T(512)(128)(4,1)}, u32[]{:S(2)}) copy-start(pred[64]{0:T(512)(128)(4,1)} %iota_compare_fusion.7) | copy-start | bytes 196
  224.1 12.3 %copy-start.18 = (pred[8]{0:T(512)(128)(4,1)S(1)}, pred[8]{0:T(512)(128)(4,1)}, u32[]{:S(2)}) copy-start(pred[8]{0:T(512)(128)(4,1)} %add_compare_fusion) | copy-start | bytes 28
  224.8 13.0 %collective-permute-start.5 = (f32[4,64,128]{2,1,0:T(8,128)S(1)}, f32[4,64,128]{2,1,0:T(8,128)S(1)}, u32[]{:S(2)}, u32[]{:S(2)}) collective-permute-start(f32[4,64,128]{2,1,0:T(8,128)S(1)} %get-tuple-element.81), channel_id=1, source_target_pairs={{0,1},{1,2},{2,3},{3,4},{4,5},{5,6},{6,7},{7,8},{8,9},{9,10},{10,1... | collective-permute-start | bytes 393224 | tf_op jit(solution)/shard_map/ppermute | solution.py:17
  234.4 10.5 %collective-permute-start.4 = (f32[4,64,128]{2,1,0:T(8,128)S(1)}, f32[4,64,128]{2,1,0:T(8,128)S(1)}, u32[]{:S(2)}, u32[]{:S(2)}) collective-permute-start(f32[4,64,128]{2,1,0:T(8,128)S(1)} %get-tuple-element.80), channel_id=1, source_target_pairs={{1,0},{2,1},{3,2},{4,3},{5,4},{6,5},{7,6},{8,7},{9,8},{10,9},{11,1... | collective-permute-start | bytes 393224 | tf_op jit(solution)/shard_map/ppermute | solution.py:18
  247.0 19.2 %copy-start.9 = (f32[512,128]{1,0:T(8,128)S(1)}, f32[512,128]{1,0:T(8,128)}, u32[]{:S(2)}) copy-start(f32[512,128]{1,0:T(8,128)} %fusion.661) | copy-start | bytes 786436
  247.2 19.0 %collective-permute-start.7 = (f32[4,64,128]{2,1,0:T(8,128)S(1)}, f32[4,64,128]{2,1,0:T(8,128)S(1)}, u32[]{:S(2)}, u32[]{:S(2)}) collective-permute-start(f32[4,64,128]{2,1,0:T(8,128)S(1)} %get-tuple-element.79), channel_id=1, source_target_pairs={{0,1},{1,2},{2,3},{3,4},{4,5},{5,6},{6,7},{7,8},{8,9},{9,10},{10,1... | collective-permute-start | bytes 393224 | tf_op jit(solution)/shard_map/ppermute | solution.py:17
  258.6 7.5 %collective-permute-start.6 = (f32[4,64,128]{2,1,0:T(8,128)S(1)}, f32[4,64,128]{2,1,0:T(8,128)S(1)}, u32[]{:S(2)}, u32[]{:S(2)}) collective-permute-start(f32[4,64,128]{2,1,0:T(8,128)S(1)} %get-tuple-element.78), channel_id=1, source_target_pairs={{1,0},{2,1},{3,2},{4,3},{5,4},{6,5},{7,6},{8,7},{9,8},{10,9},{11,1... | collective-permute-start | bytes 393224 | tf_op jit(solution)/shard_map/ppermute | solution.py:18
  260.6 16.3 %collective-permute-start.21 = (f32[4,64,128]{2,1,0:T(8,128)S(1)}, f32[4,64,128]{2,1,0:T(8,128)S(1)}, u32[]{:S(2)}, u32[]{:S(2)}) collective-permute-start(f32[4,64,128]{2,1,0:T(8,128)S(1)} %get-tuple-element.97), channel_id=1, source_target_pairs={{0,1},{1,2},{2,3},{3,4},{4,5},{5,6},{6,7},{7,8},{8,9},{9,10},{10,1... | collective-permute-start | bytes 393224 | tf_op jit(solution)/shard_map/ppermute | solution.py:17
  263.0 13.9 %collective-permute-start.20 = (f32[4,64,128]{2,1,0:T(8,128)S(1)}, f32[4,64,128]{2,1,0:T(8,128)S(1)}, u32[]{:S(2)}, u32[]{:S(2)}) collective-permute-start(f32[4,64,128]{2,1,0:T(8,128)S(1)} %get-tuple-element.96), channel_id=1, source_target_pairs={{1,0},{2,1},{3,2},{4,3},{5,4},{6,5},{7,6},{8,7},{9,8},{10,9},{11,1... | collective-permute-start | bytes 393224 | tf_op jit(solution)/shard_map/ppermute | solution.py:18
  266.9 108.0 %copy-start.7 = (f32[8,64,128]{2,1,0:T(8,128)}, f32[8,64,128]{2,1,0:T(8,128)S(1)}, u32[]{:S(2)}) copy-start(f32[8,64,128]{2,1,0:T(8,128)S(1)} %get-tuple-element.43) | copy-start | bytes 786436
  266.9 12.2 %collective-permute-start.9 = (f32[4,64,128]{2,1,0:T(8,128)S(1)}, f32[4,64,128]{2,1,0:T(8,128)S(1)}, u32[]{:S(2)}, u32[]{:S(2)}) collective-permute-start(f32[4,64,128]{2,1,0:T(8,128)S(1)} %get-tuple-element.77), channel_id=1, source_target_pairs={{0,1},{1,2},{2,3},{3,4},{4,5},{5,6},{6,7},{7,8},{8,9},{9,10},{10,1... | collective-permute-start | bytes 393224 | tf_op jit(solution)/shard_map/ppermute | solution.py:17
  274.8 10.5 %collective-permute-start.8 = (f32[4,64,128]{2,1,0:T(8,128)S(1)}, f32[4,64,128]{2,1,0:T(8,128)S(1)}, u32[]{:S(2)}, u32[]{:S(2)}) collective-permute-start(f32[4,64,128]{2,1,0:T(8,128)S(1)} %get-tuple-element.76), channel_id=1, source_target_pairs={{1,0},{2,1},{3,2},{4,3},{5,4},{6,5},{7,6},{8,7},{9,8},{10,9},{11,1... | collective-permute-start | bytes 393224 | tf_op jit(solution)/shard_map/ppermute | solution.py:18
  287.6 13.4 %collective-permute-start.23 = (f32[4,64,128]{2,1,0:T(8,128)S(1)}, f32[4,64,128]{2,1,0:T(8,128)S(1)}, u32[]{:S(2)}, u32[]{:S(2)}) collective-permute-start(f32[4,64,128]{2,1,0:T(8,128)S(1)} %get-tuple-element.95), channel_id=1, source_target_pairs={{0,1},{1,2},{2,3},{3,4},{4,5},{5,6},{6,7},{7,8},{8,9},{9,10},{10,1... | collective-permute-start | bytes 393224 | tf_op jit(solution)/shard_map/ppermute | solution.py:17
  299.1 4.4 collective-permute-start.22
  304.8 11.7 %collective-permute-start.25 = (f32[4,64,128]{2,1,0:T(8,128)S(1)}, f32[4,64,128]{2,1,0:T(8,128)S(1)}, u32[]{:S(2)}, u32[]{:S(2)}) collective-permute-start(f32[4,64,128]{2,1,0:T(8,128)S(1)} %get-tuple-element.93), channel_id=1, source_target_pairs={{0,1},{1,2},{2,3},{3,4},{4,5},{5,6},{6,7},{7,8},{8,9},{9,10},{10,1... | collective-permute-start | bytes 393224 | tf_op jit(solution)/shard_map/ppermute | solution.py:17
  314.6 4.4 collective-permute-start.24
  321.3 11.7 %collective-permute-start.27 = (f32[4,64,128]{2,1,0:T(8,128)S(1)}, f32[4,64,128]{2,1,0:T(8,128)S(1)}, u32[]{:S(2)}, u32[]{:S(2)}) collective-permute-start(f32[4,64,128]{2,1,0:T(8,128)S(1)} %get-tuple-element.91), channel_id=1, source_target_pairs={{0,1},{1,2},{2,3},{3,4},{4,5},{5,6},{6,7},{7,8},{8,9},{9,10},{10,1... | collective-permute-start | bytes 393224 | tf_op jit(solution)/shard_map/ppermute | solution.py:17
  331.1 4.4 collective-permute-start.26
  336.8 17.3 %collective-permute-start.29 = (f32[4,64,128]{2,1,0:T(8,128)S(1)}, f32[4,64,128]{2,1,0:T(8,128)S(1)}, u32[]{:S(2)}, u32[]{:S(2)}) collective-permute-start(f32[4,64,128]{2,1,0:T(8,128)S(1)} %get-tuple-element.89), channel_id=1, source_target_pairs={{0,1},{1,2},{2,3},{3,4},{4,5},{5,6},{6,7},{7,8},{8,9},{9,10},{10,1... | collective-permute-start | bytes 393224 | tf_op jit(solution)/shard_map/ppermute | solution.py:17
  346.6 7.5 %collective-permute-start.28 = (f32[4,64,128]{2,1,0:T(8,128)S(1)}, f32[4,64,128]{2,1,0:T(8,128)S(1)}, u32[]{:S(2)}, u32[]{:S(2)}) collective-permute-start(f32[4,64,128]{2,1,0:T(8,128)S(1)} %get-tuple-element.88), channel_id=1, source_target_pairs={{1,0},{2,1},{3,2},{4,3},{5,4},{6,5},{7,6},{8,7},{9,8},{10,9},{11,1... | collective-permute-start | bytes 393224 | tf_op jit(solution)/shard_map/ppermute | solution.py:18
  348.6 18.1 %collective-permute-start.11 = (f32[4,64,128]{2,1,0:T(8,128)S(1)}, f32[4,64,128]{2,1,0:T(8,128)S(1)}, u32[]{:S(2)}, u32[]{:S(2)}) collective-permute-start(f32[4,64,128]{2,1,0:T(8,128)S(1)} %get-tuple-element.75), channel_id=1, source_target_pairs={{0,1},{1,2},{2,3},{3,4},{4,5},{5,6},{6,7},{7,8},{8,9},{9,10},{10,1... | collective-permute-start | bytes 393224 | tf_op jit(solution)/shard_map/ppermute | solution.py:17
  351.0 15.7 %collective-permute-start.10 = (f32[4,64,128]{2,1,0:T(8,128)S(1)}, f32[4,64,128]{2,1,0:T(8,128)S(1)}, u32[]{:S(2)}, u32[]{:S(2)}) collective-permute-start(f32[4,64,128]{2,1,0:T(8,128)S(1)} %get-tuple-element.74), channel_id=1, source_target_pairs={{1,0},{2,1},{3,2},{4,3},{5,4},{6,5},{7,6},{8,7},{9,8},{10,9},{11,1... | collective-permute-start | bytes 393224 | tf_op jit(solution)/shard_map/ppermute | solution.py:18
  356.3 10.1 %copy-start.21 = (f32[128]{0:T(128)S(1)}, f32[128]{0:T(128)}, u32[]{:S(2)}) copy-start(f32[128]{0:T(128)} %get-tuple-element.105) | copy-start | bytes 1540
  356.4 10.3 %collective-permute-start.31 = (f32[4,64,128]{2,1,0:T(8,128)S(1)}, f32[4,64,128]{2,1,0:T(8,128)S(1)}, u32[]{:S(2)}, u32[]{:S(2)}) collective-permute-start(f32[4,64,128]{2,1,0:T(8,128)S(1)} %get-tuple-element.87), channel_id=1, source_target_pairs={{0,1},{1,2},{2,3},{3,4},{4,5},{5,6},{6,7},{7,8},{8,9},{9,10},{10,1... | collective-permute-start | bytes 393224 | tf_op jit(solution)/shard_map/ppermute | solution.py:17
  364.4 10.5 %collective-permute-start.30 = (f32[4,64,128]{2,1,0:T(8,128)S(1)}, f32[4,64,128]{2,1,0:T(8,128)S(1)}, u32[]{:S(2)}, u32[]{:S(2)}) collective-permute-start(f32[4,64,128]{2,1,0:T(8,128)S(1)} %get-tuple-element.86), channel_id=1, source_target_pairs={{1,0},{2,1},{3,2},{4,3},{5,4},{6,5},{7,6},{8,7},{9,8},{10,9},{11,1... | collective-permute-start | bytes 393224 | tf_op jit(solution)/shard_map/ppermute | solution.py:18
  377.0 34.3 %copy-start.6 = (f32[8,64,128]{2,1,0:T(8,128)}, f32[8,64,128]{2,1,0:T(8,128)S(1)}, u32[]{:S(2)}) copy-start(f32[8,64,128]{2,1,0:T(8,128)S(1)} %get-tuple-element.4) | copy-start | bytes 786436
  377.8 16.0 %collective-permute-start.13 = (f32[4,64,128]{2,1,0:T(8,128)}, f32[4,64,128]{2,1,0:T(8,128)S(1)}, u32[]{:S(2)}, u32[]{:S(2)}) collective-permute-start(f32[4,64,128]{2,1,0:T(8,128)} %get-tuple-element.73), channel_id=1, source_target_pairs={{0,1},{1,2},{2,3},{3,4},{4,5},{5,6},{6,7},{7,8},{8,9},{9,10},{10,1... | collective-permute-start | bytes 393224 | tf_op jit(solution)/shard_map/ppermute | solution.py:17
  389.2 4.7 collective-permute-start.12
  396.9 11.9 %copy-start.20 = (f32[128]{0:T(128)S(1)}, f32[128]{0:T(128)}, u32[]{:S(2)}) copy-start(f32[128]{0:T(128)} %get-tuple-element.102) | copy-start | bytes 1540
  396.9 14.4 %copy-start.8 = (f32[8,64,128]{2,1,0:T(8,128)S(1)}, f32[8,64,128]{2,1,0:T(8,128)}, u32[]{:S(2)}) copy-start(f32[8,64,128]{2,1,0:T(8,128)} %copy-done.7) | copy-start | bytes 786436
  397.1 12.1 %collective-permute-start.15 = (f32[4,64,128]{2,1,0:T(8,128)S(1)}, f32[4,64,128]{2,1,0:T(8,128)S(1)}, u32[]{:S(2)}, u32[]{:S(2)}) collective-permute-start(f32[4,64,128]{2,1,0:T(8,128)S(1)} %get-tuple-element.71), channel_id=1, source_target_pairs={{0,1},{1,2},{2,3},{3,4},{4,5},{5,6},{6,7},{7,8},{8,9},{9,10},{10,1... | collective-permute-start | bytes 393224 | tf_op jit(solution)/shard_map/ppermute | solution.py:17
  406.9 4.4 collective-permute-start.14
Sparse Core Ops, SparseCore 0:
  393.9 85.7 reduce-scatter.1
